TPU v7x, 256 devices: a whole 4x4x8 slice. The times are simulated.
256 devices in a mesh: gx: 4 (over x), gy: 8 (over y, core), gz: 8 (over z).
Axes of the slice: x: 4, y: 4, z: 8, core: 2. Of those that a mesh axis runs over, the one named last changes fastest.
Arguments:
- earlier_basis: float32 [8, 4, 16, 128, 1024], P(None, None, 'gx', 'gy', 'gz'), may hold values from -40 to 40
- diffusivity: float32 [4, 16, 128, 1024], P(None, 'gx', 'gy', 'gz'), may hold values from 0.5 to 4
- reaction: float32 [4, 4, 16, 128, 1024], P(None, None, 'gx', 'gy', 'gz'), may hold values from -4 to 4
Outputs:
- new_basis: float32 [4, 4, 16, 128, 1024], P(None, None, 'gx', 'gy', 'gz')
- coefficients: float32 [8, 4], replicated
- triangle: float32 [4, 4], replicated
All inputs are finite; a program needn't handle non-finite values.
Results may differ from a plain program's by a relative error of at most 0.00027.
Values sent between devices are 32-bit elements; how exact they have to be, the bound alone decides.
No kernel may reach another device: no remote copies, remote signals or barrier semaphores. Data moves between devices by JAX's collectives and lax.ppermute only.
A program may use at most 64 MiB of HBM per device.

v0:
```python
import jax
import jax.numpy as jnp
from jax import lax
from jax.sharding import PartitionSpec as P

SPECIES = 4
STEPS = 4
EARLIER = 8


SHIFTS = (6.0, 9.0, 14.0, 17.0)
DAMPING = 0.2
HIGHEST = lax.Precision.HIGHEST


def with_halo(block, sides, width):
    for axis, dim in sides:
        count = lax.axis_size(axis)
        forward = [(i, i + 1) for i in range(count - 1)]
        backward = [(target, source) for source, target in forward]
        low = lax.ppermute(
            lax.slice_in_dim(block, block.shape[dim] - width, None, axis=dim), axis, forward
        )
        high = lax.ppermute(lax.slice_in_dim(block, 0, width, axis=dim), axis, backward)
        block = jnp.concatenate([low, block, high], axis=dim)
    return block


def operate(padded, conduct, reaction_local):
    center = padded[:, 1:-1, 1:-1, 1:-1]
    middle = conduct[:, 1:-1, 1:-1, 1:-1]
    applied = center
    for source in range(SPECIES):
        applied = applied + reaction_local[:, source] * center[source]
    sides = [
        (padded[:, 2:, 1:-1, 1:-1], conduct[:, 2:, 1:-1, 1:-1]),
        (padded[:, :-2, 1:-1, 1:-1], conduct[:, :-2, 1:-1, 1:-1]),
        (padded[:, 1:-1, 2:, 1:-1], conduct[:, 1:-1, 2:, 1:-1]),
        (padded[:, 1:-1, :-2, 1:-1], conduct[:, 1:-1, :-2, 1:-1]),
        (padded[:, 1:-1, 1:-1, 2:], conduct[:, 1:-1, 1:-1, 2:]),
        (padded[:, 1:-1, 1:-1, :-2], conduct[:, 1:-1, 1:-1, :-2]),
    ]
    for other_value, other_conduct in sides:
        applied = applied + 0.5 * (middle + other_conduct) * (center - other_value)
    return (applied, center)


def trim(array, depth):
    return array[
        ...,
        depth : array.shape[-3] - depth,
        depth : array.shape[-2] - depth,
        depth : array.shape[-1] - depth,
    ]


def inside_range(coords, limit):
    return ((coords >= 0) & (coords < limit)).astype(jnp.float32)


def on_device(earlier_basis, diffusivity, reaction):
    span_x, span_y, span_z = (diffusivity.shape[1], diffusivity.shape[2], diffusivity.shape[3])
    columns = []
    stacked = jnp.concatenate(
        [
            earlier_basis[EARLIER - 1],
            diffusivity,
            reaction.reshape((SPECIES * SPECIES,) + diffusivity.shape[1:]),
        ],
        0,
    )
    padded = with_halo(stacked, (("gx", 1), ("gy", 2), ("gz", 3)), STEPS)
    vector = padded[:SPECIES]
    conduct_all = padded[SPECIES : 2 * SPECIES]
    reaction_all = padded[2 * SPECIES :].reshape((SPECIES, SPECIES) + padded.shape[1:])
    coord_x = lax.axis_index("gx") * span_x - STEPS + jnp.arange(span_x + 2 * STEPS)
    coord_y = lax.axis_index("gy") * span_y - STEPS + jnp.arange(span_y + 2 * STEPS)
    coord_z = lax.axis_index("gz") * span_z - STEPS + jnp.arange(span_z + 2 * STEPS)
    inside_x = inside_range(coord_x, span_x * lax.axis_size("gx"))
    inside_y = inside_range(coord_y, span_y * lax.axis_size("gy"))
    inside_z = inside_range(coord_z, span_z * lax.axis_size("gz"))
    inside_mask = inside_x[:, None, None] * inside_y[None, :, None] * inside_z[None, None, :]
    for degree in range(STEPS):
        applied, center = operate(vector, trim(conduct_all, degree), trim(reaction_all, degree + 1))
        vector = (applied - SHIFTS[degree] * center) * DAMPING * trim(inside_mask, degree + 1)
        columns.append(trim(vector, STEPS - degree - 1).reshape(-1))
    flat_block = jnp.stack(columns)
    flat_basis = earlier_basis.reshape(EARLIER, -1)
    entries = flat_basis.shape[1] * lax.axis_size("gx") * lax.axis_size("gy") * lax.axis_size("gz")
    coeffs = (
        lax.psum(jnp.dot(flat_basis, flat_block.T, precision=HIGHEST), ("gx", "gy", "gz")) / entries
    )
    residue = flat_block - jnp.dot(coeffs.T, flat_basis, precision=HIGHEST)
    block_gram = (
        lax.psum(jnp.dot(residue, residue.T, precision=HIGHEST), ("gx", "gy", "gz")) / entries
    )
    factor = jnp.linalg.cholesky(block_gram)
    renewed = lax.linalg.triangular_solve(factor, residue, left_side=True, lower=True)
    return (renewed.reshape((STEPS,) + diffusivity.shape), coeffs, factor.T)


def solution(mesh):
    in_specs = (
        P(None, None, "gx", "gy", "gz"),
        P(None, "gx", "gy", "gz"),
        P(None, None, "gx", "gy", "gz"),
    )
    out_specs = (P(None, None, "gx", "gy", "gz"), P(), P())
    return jax.shard_map(
        on_device, mesh=mesh, in_specs=in_specs, out_specs=out_specs, check_vma=False
    )
```

profile of v0, /device:TPU:1, one launch (start us, length us, event | category | flops | bytes accessed | tf_op | source)
XLA Modules:
  0.0 280.7 jit_solution(18112395164197896029)
XLA Ops:
  2.8 4.0 %collective-permute-start = (f32[24,4,16,128]{3,2,1,0:T(8,128)S(1)}, f32[24,4,16,128]{3,2,1,0:T(8,128)S(1)}, u32[]{:S(2)}, u32[]{:S(2)}) collective-permute-start(f32[24,4,16,128]{3,2,1,0:T(8,128)S(1)} %pad_maximum_fusion.3), channel_id=1, source_target_pairs={{0,64},{64,128},{128,192},{1,65},{65,129},{129,193},{2,66},{66,130... | collective-permute-start | bytes 2359304 | tf_op jit(solution)/shard_map/ppermute | solution.py:21
  8.3 14.6 %collective-permute-done = f32[24,4,16,128]{3,2,1,0:T(8,128)S(1)} collective-permute-done((f32[24,4,16,128]{3,2,1,0:T(8,128)S(1)}, f32[24,4,16,128]{3,2,1,0:T(8,128)S(1)}, u32[]{:S(2)}, u32[]{:S(2)}) %collective-permute-start) | collective-permute-done | bytes 786464 | tf_op jit(solution)/shard_map/ppermute | solution.py:21
  22.9 3.9 %collective-permute-done.1 = f32[24,4,16,128]{3,2,1,0:T(8,128)S(1)} collective-permute-done((f32[24,4,16,128]{3,2,1,0:T(8,128)S(1)}, f32[24,4,16,128]{3,2,1,0:T(8,128)S(1)}, u32[]{:S(2)}, u32[]{:S(2)}) %collective-permute-start.1) | collective-permute-done | bytes 786464 | tf_op jit(solution)/shard_map/ppermute | solution.py:24
  28.4 4.9 %collective-permute-start.2 = (f32[24,12,4,128]{3,2,1,0:T(4,128)S(1)}, f32[24,12,4,128]{3,2,1,0:T(4,128)S(1)}, u32[]{:S(2)}, u32[]{:S(2)}) collective-permute-start(f32[24,12,4,128]{3,2,1,0:T(4,128)S(1)} %get-tuple-element.20), channel_id=1, source_target_pairs={{0,8},{8,16},{16,24},{24,32},{32,40},{40,48},{48,56},{1,9},{9,17},... | collective-permute-start | bytes 1769480 | tf_op jit(solution)/shard_map/ppermute | solution.py:21
  33.3 1.9 collective-permute-start.3
  37.6 2.5 collective-permute-done.2
  40.1 4.4 %collective-permute-done.3 = f32[24,12,4,128]{3,2,1,0:T(4,128)S(1)} collective-permute-done((f32[24,12,4,128]{3,2,1,0:T(4,128)S(1)}, f32[24,12,4,128]{3,2,1,0:T(4,128)S(1)}, u32[]{:S(2)}, u32[]{:S(2)}) %collective-permute-start.3) | collective-permute-done | bytes 589856 | tf_op jit(solution)/shard_map/ppermute | solution.py:24
  46.9 4.1 %fusion.125 = (f32[24,12,24,4]{3,2,1,0:T(8,128)}, f32[24,12,24,4]{3,2,1,0:T(8,128)}) fusion(f32[24,12,24,128]{3,2,1,0:T(8,128)S(1)} %pad_maximum_fusion.2), kind=kLoop, calls=%fused_computation.249 | loop fusion | bytes 442368 | tf_op jit(solution)/shard_map/slice | solution.py:22
  51.0 3.4 %copy.33 = f32[24,12,24,4]{2,0,3,1:T(8,128)S(1)} copy(f32[24,12,24,4]{3,2,1,0:T(8,128)} %get-tuple-element.18) | data formatting | bytes 221184 | tf_op jit(solution)/shard_map/slice | solution.py:22
  54.4 4.4 %collective-permute-start.4 = (f32[24,12,24,4]{2,0,3,1:T(8,128)S(1)}, f32[24,12,24,4]{2,0,3,1:T(8,128)}, u32[]{:S(2)}, u32[]{:S(2)}) collective-permute-start(f32[24,12,24,4]{2,0,3,1:T(8,128)S(1)} %copy.33), channel_id=1, source_target_pairs={{0,1},{1,2},{2,3},{3,4},{4,5},{5,6},{6,7},{8,9},{9,10},{10,11},{11... | collective-permute-start | bytes 331784 | tf_op jit(solution)/shard_map/ppermute | solution.py:21
  58.7 4.1 %copy.34 = f32[24,12,24,4]{2,0,3,1:T(8,128)} copy(f32[24,12,24,4]{3,2,1,0:T(8,128)} %get-tuple-element.19) | data formatting | bytes 221184 | tf_op jit(solution)/shard_map/slice | solution.py:24
  65.0 2.8 copy.35
  67.7 6.0 %collective-permute-done.5 = f32[24,12,24,4]{2,0,3,1:T(8,128)} collective-permute-done((f32[24,12,24,4]{2,0,3,1:T(8,128)}, f32[24,12,24,4]{2,0,3,1:T(8,128)}, u32[]{:S(2)}, u32[]{:S(2)}) %collective-permute-start.5) | collective-permute-done | bytes 110624 | tf_op jit(solution)/shard_map/ppermute | solution.py:24
  73.7 4.0 %copy.36 = f32[24,12,24,4]{3,2,1,0:T(8,128)} copy(f32[24,12,24,4]{2,0,3,1:T(8,128)} %collective-permute-done.5) | data formatting | bytes 221184 | tf_op jit(solution)/shard_map/ppermute | solution.py:24
  77.7 9.4 %pad_maximum_fusion = f32[24,12,24,136]{3,2,1,0:T(8,128)S(1)} fusion(f32[24,12,24,4]{3,2,1,0:T(8,128)} %copy.36, f32[24,12,4,128]{3,2,1,0:T(4,128)} %copy-done.9, f32[24,4,16,128]{3,2,1,0:T(8,128)} %copy-done.3, f32[16,4,16,128]{3,2,1,0:T(8,128)} %bitcast.236, f32[4,4,16,128]{3,2,1,0:T(8,128)} %param.4, f32[4,4,16,128]{3,2,1,0:T(8,128)} %copy-done.11, ...), kind=kLoop, calls=%fused_computation.1 | loop fusion | flops 7520256 | bytes 7520256 | tf_op jit(solution)/shard_map/concatenate | solution.py:25
  88.1 4.3 %fusion.7 = f32[4,10,22,134]{3,2,1,0:T(8,128)S(1)} fusion(f32[24,12,24,136]{3,2,1,0:T(8,128)S(1)} %pad_maximum_fusion, f32[4,4,12,24,136]{4,3,2,1,0:T(8,128)S(1)} %bitcast.230, f32[10,22,134]{2,1,0:T(8,128)S(1)} %copy-done.14, f32[10,22,134]{2,1,0:T(8,128)S(1)} %get-tuple-element.13, f32[10,22,134]{2,1,0:T(8,128)S(1)} %get-tuple-element.14, ...), kind=kLoop, calls=%fused_computation.14 | loop fusion | flops 4834720 | bytes 9551520 | tf_op jit(solution)/shard_map/mul | solution.py:85
  92.8 3.8 %fusion.35 = f32[4,8,20,132]{3,2,1,0:T(8,128)S(1)} fusion(f32[4,10,22,134]{3,2,1,0:T(8,128)S(1)} %fusion.7, f32[24,12,24,136]{3,2,1,0:T(8,128)S(1)} %pad_maximum_fusion, f32[4,4,12,24,136]{4,3,2,1,0:T(8,128)S(1)} %bitcast.231, f32[8,20,132]{2,1,0:T(8,128)S(1)} %copy-done.15, f32[8,20,132]{2,1,0:T(8,128)S(1)} %get-tuple-element.23, ...), kind=kLoop, calls=%fused_computation.58 | loop fusion | flops 3463680 | bytes 6842880 | tf_op jit(solution)/shard_map/mul | solution.py:85
  96.9 9.7 %pad_maximum_fusion.1 = (f32[24,12,24,132]{3,2,1,0:T(8,128)}, f32[24,12,24,132]{3,2,1,0:T(8,128)}) fusion(f32[24,12,24,4]{3,2,1,0:T(8,128)S(1)} %copy-done, f32[24,12,4,128]{3,2,1,0:T(4,128)S(1)} %copy-done.10, f32[24,4,16,128]{3,2,1,0:T(8,128)S(1)} %copy-done.4, f32[16,4,16,128]{3,2,1,0:T(8,128)S(1)} %bitcast.238, f32[4,4,16,128]{3,2,1,0:T(8,128)S(1)} %copy-done.13, ...), kind=kLoop, calls=%fused_computation.2 | loop fusion | flops 12773376 | bytes 11059200 | tf_op jit(solution)/shard_map/concatenate | solution.py:25
  106.6 3.9 %fusion.63 = f32[4,6,18,130]{3,2,1,0:T(8,128)S(1)} fusion(f32[4,8,20,132]{3,2,1,0:T(8,128)S(1)} %fusion.35, f32[24,12,24,132]{3,2,1,0:T(8,128)} %get-tuple-element.17, f32[24,12,24,132]{3,2,1,0:T(8,128)} %get-tuple-element.16, f32[24,12,24,136]{3,2,1,0:T(8,128)S(1)} %pad_maximum_fusion, f32[4,4,12,24,136]{4,3,2,1,0:T(8,128)S(1)} %bitcast.232, ...), kind=kLoop, calls=%fused_computation.103 | loop fusion | flops 2302560 | bytes 4548960 | tf_op jit(solution)/shard_map/mul | solution.py:85
  112.6 2.7 convolution_bitcast_fusion
  115.3 83.7 %psum.14 = f32[8,4]{0,1:T(4,128)S(1)} all-reduce(f32[8,4]{0,1:T(4,128)S(1)} %convolution_bitcast_fusion), channel_id=1, replica_groups=mesh['gx'=4,'gy'=8,'gz'=8] {'gx','gy','gz'}, use_global_device_ids=true, to_apply=%region_0.0 | all-reduce | flops 32 | bytes 256 | tf_op jit(solution)/shard_map/psum | solution.py:91
  199.0 1.9 convolution_subtract_fusion
  200.9 2.3 fusion.126
  203.2 72.6 %psum.15 = f32[4,4]{0,1:T(4,128)S(1)} all-reduce(f32[4,4]{0,1:T(4,128)S(1)} %fusion.126), channel_id=1, replica_groups=mesh['gx'=4,'gy'=8,'gz'=8] {'gx','gy','gz'}, use_global_device_ids=true, to_apply=%region_1.0 | all-reduce | flops 16 | bytes 128 | tf_op jit(solution)/shard_map/psum | solution.py:95
  (77 shorter events, 20.5 us)
Async XLA Ops:
  0.6 44.7 %copy-start.5 = (f32[4,4,4,16,128]{4,3,2,1,0:T(8,128)S(1)}, f32[4,4,4,16,128]{4,3,2,1,0:T(8,128)}, u32[]{:S(2)}) copy-start(f32[4,4,4,16,128]{4,3,2,1,0:T(8,128)} %param.5) | copy-start | bytes 1572868
  1.6 49.4 %copy-start.11 = (f32[4,4,16,128]{3,2,1,0:T(8,128)}, f32[4,4,16,128]{3,2,1,0:T(8,128)S(1)}, u32[]{:S(2)}) copy-start(f32[4,4,16,128]{3,2,1,0:T(8,128)S(1)} %slice_bitcast_fusion.28) | copy-start | bytes 393220
  2.8 20.1 %collective-permute-start = (f32[24,4,16,128]{3,2,1,0:T(8,128)S(1)}, f32[24,4,16,128]{3,2,1,0:T(8,128)S(1)}, u32[]{:S(2)}, u32[]{:S(2)}) collective-permute-start(f32[24,4,16,128]{3,2,1,0:T(8,128)S(1)} %pad_maximum_fusion.3), channel_id=1, source_target_pairs={{0,64},{64,128},{128,192},{1,65},{65,129},{129,193},{2,66},{66,130... | collective-permute-start | bytes 2359304 | tf_op jit(solution)/shard_map/ppermute | solution.py:21
  6.8 20.0 %collective-permute-start.1 = (f32[24,4,16,128]{3,2,1,0:T(8,128)S(1)}, f32[24,4,16,128]{3,2,1,0:T(8,128)S(1)}, u32[]{:S(2)}, u32[]{:S(2)}) collective-permute-start(f32[24,4,16,128]{3,2,1,0:T(8,128)S(1)} %pad_maximum_fusion.3), channel_id=1, source_target_pairs={{64,0},{128,64},{192,128},{65,1},{129,65},{193,129},{66,2},{130,66... | collective-permute-start | bytes 2359304 | tf_op jit(solution)/shard_map/ppermute | solution.py:24
  22.9 28.0 %copy-start.1 = (f32[24,4,16,128]{3,2,1,0:T(8,128)}, f32[24,4,16,128]{3,2,1,0:T(8,128)S(1)}, u32[]{:S(2)}) copy-start(f32[24,4,16,128]{3,2,1,0:T(8,128)S(1)} %collective-permute-done) | copy-start | bytes 2359300
  26.8 24.1 %copy-start.3 = (f32[24,4,16,128]{3,2,1,0:T(8,128)}, f32[24,4,16,128]{3,2,1,0:T(8,128)S(1)}, u32[]{:S(2)}) copy-start(f32[24,4,16,128]{3,2,1,0:T(8,128)S(1)} %collective-permute-done.1) | copy-start | bytes 2359300
  28.4 11.7 %collective-permute-start.2 = (f32[24,12,4,128]{3,2,1,0:T(4,128)S(1)}, f32[24,12,4,128]{3,2,1,0:T(4,128)S(1)}, u32[]{:S(2)}, u32[]{:S(2)}) collective-permute-start(f32[24,12,4,128]{3,2,1,0:T(4,128)S(1)} %get-tuple-element.20), channel_id=1, source_target_pairs={{0,8},{8,16},{16,24},{24,32},{32,40},{40,48},{48,56},{1,9},{9,17},... | collective-permute-start | bytes 1769480 | tf_op jit(solution)/shard_map/ppermute | solution.py:21
  33.3 11.2 %collective-permute-start.3 = (f32[24,12,4,128]{3,2,1,0:T(4,128)S(1)}, f32[24,12,4,128]{3,2,1,0:T(4,128)S(1)}, u32[]{:S(2)}, u32[]{:S(2)}) collective-permute-start(f32[24,12,4,128]{3,2,1,0:T(4,128)S(1)} %get-tuple-element.21), channel_id=1, source_target_pairs={{8,0},{16,8},{24,16},{32,24},{40,32},{48,40},{56,48},{9,1},{17,9},... | collective-permute-start | bytes 1769480 | tf_op jit(solution)/shard_map/ppermute | solution.py:24
  40.1 4.4 %copy-start.7 = (f32[24,12,4,128]{3,2,1,0:T(4,128)}, f32[24,12,4,128]{3,2,1,0:T(4,128)S(1)}, u32[]{:S(2)}) copy-start(f32[24,12,4,128]{3,2,1,0:T(4,128)S(1)} %collective-permute-done.2) | copy-start | bytes 1769476
  54.4 10.6 %collective-permute-start.4 = (f32[24,12,24,4]{2,0,3,1:T(8,128)S(1)}, f32[24,12,24,4]{2,0,3,1:T(8,128)}, u32[]{:S(2)}, u32[]{:S(2)}) collective-permute-start(f32[24,12,24,4]{2,0,3,1:T(8,128)S(1)} %copy.33), channel_id=1, source_target_pairs={{0,1},{1,2},{2,3},{3,4},{4,5},{5,6},{6,7},{8,9},{9,10},{10,11},{11... | collective-permute-start | bytes 331784 | tf_op jit(solution)/shard_map/ppermute | solution.py:21
  62.8 10.9 %collective-permute-start.5 = (f32[24,12,24,4]{2,0,3,1:T(8,128)}, f32[24,12,24,4]{2,0,3,1:T(8,128)}, u32[]{:S(2)}, u32[]{:S(2)}) collective-permute-start(f32[24,12,24,4]{2,0,3,1:T(8,128)} %copy.34), channel_id=1, source_target_pairs={{1,0},{2,1},{3,2},{4,3},{5,4},{6,5},{7,6},{9,8},{10,9},{11,10},{12... | collective-permute-start | bytes 331784 | tf_op jit(solution)/shard_map/ppermute | solution.py:24
  88.1 4.6 %copy-start.15 = (f32[8,20,132]{2,1,0:T(8,128)S(1)}, f32[8,20,132]{2,1,0:T(8,128)}, u32[]{:S(2)}) copy-start(f32[8,20,132]{2,1,0:T(8,128)} %slice_multiply_fusion.1) | copy-start | bytes 253444
  92.7 4.1 %copy-start = (f32[24,12,24,4]{3,2,1,0:T(8,128)S(1)}, f32[24,12,24,4]{3,2,1,0:T(8,128)}, u32[]{:S(2)}) copy-start(f32[24,12,24,4]{3,2,1,0:T(8,128)} %copy.36) | copy-start | bytes 331780
  92.7 4.1 %copy-start.2 = (f32[24,4,16,128]{3,2,1,0:T(8,128)S(1)}, f32[24,4,16,128]{3,2,1,0:T(8,128)}, u32[]{:S(2)}) copy-start(f32[24,4,16,128]{3,2,1,0:T(8,128)} %copy-done.1) | copy-start | bytes 2359300
  92.7 4.1 %copy-start.4 = (f32[24,4,16,128]{3,2,1,0:T(8,128)S(1)}, f32[24,4,16,128]{3,2,1,0:T(8,128)}, u32[]{:S(2)}) copy-start(f32[24,4,16,128]{3,2,1,0:T(8,128)} %copy-done.3) | copy-start | bytes 2359300
  92.8 4.1 %copy-start.6 = (f32[4,4,4,16,128]{4,3,2,1,0:T(8,128)S(1)}, f32[4,4,4,16,128]{4,3,2,1,0:T(8,128)}, u32[]{:S(2)}) copy-start(f32[4,4,4,16,128]{4,3,2,1,0:T(8,128)} %param.5) | copy-start | bytes 1572868
  92.8 4.1 %copy-start.8 = (f32[24,12,4,128]{3,2,1,0:T(4,128)S(1)}, f32[24,12,4,128]{3,2,1,0:T(4,128)}, u32[]{:S(2)}) copy-start(f32[24,12,4,128]{3,2,1,0:T(4,128)} %copy-done.7) | copy-start | bytes 1769476
  92.8 4.1 %copy-start.10 = (f32[24,12,4,128]{3,2,1,0:T(4,128)S(1)}, f32[24,12,4,128]{3,2,1,0:T(4,128)}, u32[]{:S(2)}) copy-start(f32[24,12,4,128]{3,2,1,0:T(4,128)} %copy-done.9) | copy-start | bytes 1769476
  92.8 4.1 %copy-start.12 = (f32[4,4,16,128]{3,2,1,0:T(8,128)S(1)}, f32[4,4,16,128]{3,2,1,0:T(8,128)}, u32[]{:S(2)}) copy-start(f32[4,4,16,128]{3,2,1,0:T(8,128)} %copy-done.11) | copy-start | bytes 393220
  92.8 4.1 %copy-start.13 = (f32[4,4,16,128]{3,2,1,0:T(8,128)S(1)}, f32[4,4,16,128]{3,2,1,0:T(8,128)}, u32[]{:S(2)}) copy-start(f32[4,4,16,128]{3,2,1,0:T(8,128)} %param.4) | copy-start | bytes 393220
  96.9 9.7 %copy-start.16 = (f32[6,18,130]{2,1,0:T(8,128)S(1)}, f32[6,18,130]{2,1,0:T(8,128)}, u32[]{:S(2)}) copy-start(f32[6,18,130]{2,1,0:T(8,128)} %slice_multiply_fusion.2) | copy-start | bytes 168484
  106.6 4.3 %copy-start.17 = (f32[4,16,128]{2,1,0:T(8,128)S(1)}, f32[4,16,128]{2,1,0:T(8,128)}, u32[]{:S(2)}) copy-start(f32[4,16,128]{2,1,0:T(8,128)} %slice_multiply_fusion.3) | copy-start | bytes 98308
  106.6 6.0 %copy-start.18 = (f32[8,4,4,16,128]{4,3,2,1,0:T(8,128)S(1)}, f32[8,4,4,16,128]{4,3,2,1,0:T(8,128)}, u32[]{:S(2)}) copy-start(f32[8,4,4,16,128]{4,3,2,1,0:T(8,128)} %param.3) | copy-start | bytes 3145732
  199.0 81.7 %copy-start.19 = (f32[8,4]{0,1:T(4,128)}, f32[8,4]{0,1:T(4,128)S(1)}, u32[]{:S(2)}) copy-start(f32[8,4]{0,1:T(4,128)S(1)} %broadcast_multiply_fusion.3) | copy-start | bytes 388
  (2 other events, 1.8 us)
where the time goes:
time: 281 us
  blocking collectives  156 us (56%)
  other arithmetic  42.2 us (15%)
  waiting for transfers between devices  31.4 us (11%)
  local copies, waits for them, and re-layouts  23.7 us (8%)
  starting transfers between devices  17.9 us (6%)
  matrix products  8.16 us (3%)
    psum x1, blocking collectives, on_device(): lax.psum(jnp.dot(flat_basis, flat_block.T, precision=HIGHEST), ('gx', 'gy...  83.7 us
    psum x1, blocking collectives, on_device(): lax.psum(jnp.dot(residue, residue.T, precision=HIGHEST), ('gx', 'gy', 'gz'))  72.6 us
    concatenate x3, other arithmetic, with_halo(): block = jnp.concatenate([low, block, high], axis=dim)  20.6 us
    ppermute x3, waiting for transfers between devices, with_halo(): lax.ppermute(lax.slice_in_dim(block, block.shape[dim] - width, None, axis...  17.1 us
    mul x8, other arithmetic, on_device(): (applied - SHIFTS[degree] * center) * DAMPING  16.7 us
    ppermute x3, waiting for transfers between devices, with_halo(): lax.ppermute(lax.slice_in_dim(block, 0, width, axis=dim), axis, backward)  14.3 us
    ppermute x3, starting transfers between devices, with_halo(): lax.ppermute(lax.slice_in_dim(block, block.shape[dim] - width, None, axis...  13.3 us
    slice x2, local copies, waits for them, and re-layouts, with_halo(): lax.slice_in_dim(block, block.shape[dim] - width, None, axis=dim)  7.45 us
  transfers between devices with their start and end apart: 6, of which 5 were waited for; matrix products, arithmetic and copies ran while one was open for 4% of the time, Pallas kernels for 0%

commit v1 on v0

v1 whole, which is shorter than its diff:
```python
import functools

import jax
import jax.numpy as jnp
from jax import lax
from jax.experimental import pallas as pl
from jax.experimental.pallas import tpu as pltpu
from jax.sharding import PartitionSpec as P

SPECIES = 4
STEPS = 4
EARLIER = 8
SHIFTS = (6.0, 9.0, 14.0, 17.0)
DAMPING = 0.2
AXES = ("gx", "gy", "gz")

VECTORS = EARLIER + STEPS
SLOT = {}
for _b in range(VECTORS):
    for _a in range(_b + 1):
        SLOT[(_a, _b)] = len(SLOT)


def pack_faces(planes, x_lo, x_hi, y_lo, y_hi, z_lo, z_hi, first):
    span_x, span_y, span_z = planes[0].shape
    lane = lax.broadcasted_iota(jnp.int32, (span_y, span_z), 1)
    low, high = z_lo, z_hi
    for number, value in enumerate(planes):
        field = first + number
        x_lo[field] = value[0]
        x_hi[field] = value[span_x - 1]
        for x in range(span_x):
            k = field * span_x + x
            y_lo[k : k + 1, :] = value[x, 0:1, :]
            y_hi[k : k + 1, :] = value[x, span_y - 1 : span_y, :]
            shift_low, shift_high = k % span_z, (k + 1) % span_z
            to_low = pltpu.roll(value[x], shift_low, 1) if shift_low else value[x]
            to_high = pltpu.roll(value[x], shift_high, 1) if shift_high else value[x]
            low = jnp.where(lane == k, to_low, low)
            high = jnp.where(lane == k, to_high, high)
    return low, high


def first_faces(v_ref, d_ref, xl, xh, yl, yh, zl, zh):
    zero = jnp.zeros(zl.shape, jnp.float32)
    low, high = pack_faces([v_ref[0, s] for s in range(SPECIES)], xl, xh, yl, yh, zero, zero, 0)
    low, high = pack_faces([d_ref[s] for s in range(SPECIES)], xl, xh, yl, yh, low, high, SPECIES)
    zl[...] = low
    zh[...] = high


def edges():
    flags = []
    for axis in AXES:
        index = lax.axis_index(axis)
        flags += [index == 0, index == lax.axis_size(axis) - 1]
    return flags


def neighbours(value, halos, flags, field):
    span_x, span_y, span_z = value.shape
    xl, xh, yl, yh, zl, zh = halos
    k = field * span_x
    row = lax.broadcasted_iota(jnp.int32, value.shape, 1)
    lane = lax.broadcasted_iota(jnp.int32, value.shape, 2)

    def inside(flag, halo):
        return jnp.where(flag, jnp.zeros_like(halo), halo)

    before_x = jnp.concatenate([inside(flags[0], xl[field])[None], value[:-1]], 0)
    after_x = jnp.concatenate([value[1:], inside(flags[1], xh[field])[None]], 0)
    low_y = inside(flags[2], yl[k : k + span_x, :])[:, None, :]
    high_y = inside(flags[3], yh[k : k + span_x, :])[:, None, :]
    before_y = jnp.where(row == 0, low_y, pltpu.roll(value, 1, 1))
    after_y = jnp.where(row == span_y - 1, high_y, pltpu.roll(value, span_y - 1, 1))
    low_z, high_z = inside(flags[4], zl[...]), inside(flags[5], zh[...])

    def moved(face, shift):
        shift %= span_z
        return pltpu.roll(face, shift, 1) if shift else face

    low_z = jnp.stack([moved(low_z, -(k + x)) for x in range(span_x)])
    high_z = jnp.stack([moved(high_z, span_z - 1 - (k + x)) for x in range(span_x)])
    before_z = jnp.where(lane == 0, low_z, pltpu.roll(value, 1, 2))
    after_z = jnp.where(lane == span_z - 1, high_z, pltpu.roll(value, span_z - 1, 2))
    return before_x, after_x, before_y, after_y, before_z, after_z


def apply_operator(degree, v_of, d_ref, r_ref, d_halos, v_halos, store):
    flags = edges()
    for s in range(SPECIES):
        v = v_of(s)
        d = d_ref[s]
        applied = v * (1.0 - SHIFTS[degree])
        for t in range(SPECIES):
            applied = applied + r_ref[s, t] * v_of(t)
        near_v = neighbours(v, v_halos, flags, s)
        near_d = neighbours(d, d_halos, flags, SPECIES + s)
        for other_v, other_d in zip(near_v, near_d):
            applied = applied + (0.5 * (d + other_d)) * (v - other_v)
        store(s, applied * DAMPING)


def step_kernel(degree, *refs):
    v_ref, d_ref, r_ref = refs[:3]
    d_halos = refs[3:9]
    v_halos = d_halos if degree == 0 else refs[9:15]
    rest = refs[9:] if degree == 0 else refs[15:]
    out_ref, xl, xh, yl, yh, zl, zh = rest
    v_of = (lambda s: v_ref[0, s]) if degree == 0 else (lambda s: v_ref[s])

    def store(s, value):
        out_ref[s] = value

    apply_operator(degree, v_of, d_ref, r_ref, d_halos, v_halos, store)
    zero = jnp.zeros(zl.shape, jnp.float32)
    low, high = pack_faces([out_ref[s] for s in range(SPECIES)], xl, xh, yl, yh, zero, zero, 0)
    zl[...] = low
    zh[...] = high


def products(pairs, load, count):
    def body(i, sums):
        values = load(i)
        return tuple(total + values[a] * values[b] for total, (a, b) in zip(sums, pairs))

    zero = jnp.zeros((8, 128), jnp.float32)
    sums = lax.fori_loop(0, count, body, (zero,) * len(pairs))
    lane = lax.broadcasted_iota(jnp.int32, (8, 128), 1)
    row = zero
    for total, pair in zip(sums, pairs):
        row = jnp.where(lane == SLOT[pair], jnp.sum(total, 1, keepdims=True), row)
    return row


def earlier_products(q_ref, out_ref):
    pairs = [(a, b) for b in range(EARLIER) for a in range(b + 1)]
    out_ref[...] = products(pairs, lambda i: [q_ref[a, i] for a in range(EARLIER)], q_ref.shape[1])


def new_pairs(number):
    return [(a, EARLIER + number) for a in range(EARLIER + number + 1)]


def new_products(number, q_ref, *refs):
    v_refs, (before_ref, out_ref) = refs[: number + 1], refs[number + 1 :]

    def load(i):
        return [q_ref[a, i] for a in range(EARLIER)] + [v[i] for v in v_refs]

    out_ref[...] = before_ref[...] + products(new_pairs(number), load, q_ref.shape[1])


def last_kernel(*refs):
    v_ref, d_ref, r_ref = refs[:3]
    d_halos, v_halos = refs[3:9], refs[9:15]
    q_ref, v1, v2, before_ref, out_ref, sums_ref = refs[15:]
    span_x, span_y, span_z = d_ref.shape[1:]
    count = q_ref.shape[1]

    def store(s, value):
        per = span_x * span_y // 8
        out_ref[s * per : (s + 1) * per] = value.reshape(per, 8, span_z)

    apply_operator(STEPS - 1, lambda s: v_ref[s], d_ref, r_ref, d_halos, v_halos, store)
    v3 = v_ref.reshape(count, 8, span_z)

    def load(i):
        return [q_ref[a, i] for a in range(EARLIER)] + [v1[i], v2[i], v3[i], out_ref[i]]

    row = before_ref[...] + products(new_pairs(STEPS - 1), load, count)
    sums_ref[...] = jnp.broadcast_to(jnp.sum(row, 0, keepdims=True), sums_ref.shape)


def finish_kernel(entries, sums_ref, q_ref, *refs):
    v_refs, (new_ref, coeff_ref, triangle_ref) = refs[:STEPS], refs[STEPS:]
    total = sums_ref[0]
    for i in range(1, sums_ref.shape[0]):
        total = total + sums_ref[i]
    total = jnp.broadcast_to(jnp.sum(total, 0, keepdims=True), total.shape) * (1.0 / entries)

    def entry(a, b):
        k = SLOT[(min(a, b), max(a, b))]
        return jnp.broadcast_to(total[:, k : k + 1], total.shape)

    coeff = [[entry(i, EARLIER + j) for j in range(STEPS)] for i in range(EARLIER)]
    overlap = {(a, b): entry(a, b) for b in range(EARLIER) for a in range(b + 1)}
    gram = {}
    for k in range(STEPS):
        mixed = []
        for i in range(EARLIER):
            term = -2.0 * coeff[i][k]
            for m in range(EARLIER):
                term = term + overlap[(min(i, m), max(i, m))] * coeff[m][k]
            mixed.append(term)
        for j in range(k, STEPS):
            value = entry(EARLIER + k, EARLIER + j)
            for i in range(EARLIER):
                value = value + coeff[i][j] * mixed[i]
            gram[(j, k)] = value
    factor, inverse = {}, []
    for k in range(STEPS):
        pivot = gram[(k, k)]
        for m in range(k):
            pivot = pivot - factor[(k, m)] * factor[(k, m)]
        factor[(k, k)] = jnp.sqrt(pivot)
        inverse.append(1.0 / factor[(k, k)])
        for j in range(k + 1, STEPS):
            value = gram[(j, k)]
            for m in range(k):
                value = value - factor[(j, m)] * factor[(k, m)]
            factor[(j, k)] = value * inverse[k]
    row = lax.broadcasted_iota(jnp.int32, total.shape, 0)
    lane = lax.broadcasted_iota(jnp.int32, total.shape, 1)
    table = jnp.zeros_like(total)
    for i in range(EARLIER):
        for j in range(STEPS):
            table = jnp.where((row == i) & (lane == j), coeff[i][j], table)
    coeff_ref[...] = table[:, :STEPS]
    table = jnp.zeros_like(total)
    for (j, k), value in factor.items():
        table = jnp.where((row == k) & (lane == j), value, table)
    triangle_ref[...] = table[:STEPS, :STEPS]

    def body(n, carry):
        earlier = [q_ref[i, n] for i in range(EARLIER)]
        done = []
        for j in range(STEPS):
            value = v_refs[j][n]
            for i in range(EARLIER):
                value = value - coeff[i][j] * earlier[i]
            for k in range(j):
                value = value - factor[(j, k)] * done[k]
            done.append(value * inverse[j])
            new_ref[j, n] = done[j]
        return carry

    lax.fori_loop(0, q_ref.shape[1], body, 0)


def call(body, outs, cost, *args, **more):
    return pl.pallas_call(
        body,
        out_shape=[jax.ShapeDtypeStruct(shape, jnp.float32) for shape in outs],
        cost_estimate=pl.CostEstimate(flops=cost, bytes_accessed=cost, transcendentals=0),
        compiler_params=pltpu.CompilerParams(vmem_limit_bytes=8 << 20),
        **more,
    )(*args)


def exchange(faces):
    halos = []
    for number, axis in enumerate(AXES):
        count = lax.axis_size(axis)
        up = [(i, (i + 1) % count) for i in range(count)]
        down = [(target, source) for source, target in up]
        low, high = faces[2 * number : 2 * number + 2]
        halos += [lax.ppermute(high, axis, up), lax.ppermute(low, axis, down)]
    return halos


def on_device(earlier_basis, diffusivity, reaction):
    block = diffusivity.shape[1:]
    span_x, span_y, span_z = block
    tiles = SPECIES * span_x * span_y // 8
    devices = 1
    for axis in AXES:
        devices *= lax.axis_size(axis)
    entries = tiles * 8 * span_z * devices
    field = (SPECIES,) + block
    whole = pl.BlockSpec(memory_space=pltpu.VMEM)
    start = pl.BlockSpec((1,) + field, lambda i: (EARLIER - 1, 0, 0, 0, 0))

    def shapes(fields):
        plane, rows = (fields, span_y, span_z), (fields * span_x, span_z)
        return [plane, plane, rows, rows, (span_y, span_z), (span_y, span_z)]

    def spec_of(shape):
        return pl.BlockSpec(shape, lambda i: (0,) * len(shape))

    small = shapes(2 * SPECIES)
    faces = call(
        first_faces,
        small,
        1 << 20,
        earlier_basis,
        diffusivity,
        grid=(1,),
        in_specs=[start, spec_of(field)],
        out_specs=[spec_of(s) for s in small],
    )
    first_halos = exchange(faces)
    basis = earlier_basis.reshape(EARLIER, tiles, 8, span_z)
    (sums,) = call(earlier_products, [(8, span_z)], 4 << 20, basis)
    outs = [field] + shapes(SPECIES)
    out = call(
        functools.partial(step_kernel, 0),
        outs,
        1 << 20,
        earlier_basis,
        diffusivity,
        reaction,
        *first_halos,
        grid=(1,),
        in_specs=[start, spec_of(field), spec_of(reaction.shape)] + [spec_of(s) for s in small],
        out_specs=[spec_of(s) for s in outs],
    )
    columns = []
    for degree in range(1, STEPS):
        vector, halos = out[0], exchange(out[1:])
        columns.append(vector.reshape(tiles, 8, span_z))
        (sums,) = call(
            functools.partial(new_products, degree - 1),
            [(8, span_z)],
            4 << 20,
            basis,
            *columns,
            sums,
        )
        if degree < STEPS - 1:
            out = call(
                functools.partial(step_kernel, degree),
                outs,
                1 << 20,
                vector,
                diffusivity,
                reaction,
                *first_halos,
                *halos,
            )
    last, rows = call(
        last_kernel,
        [(tiles, 8, span_z), (devices, span_z)],
        1 << 20,
        vector,
        diffusivity,
        reaction,
        *first_halos,
        *halos,
        basis,
        columns[0],
        columns[1],
        sums,
    )
    columns.append(last)
    rows = lax.all_to_all(rows.reshape(devices, 1, span_z), AXES, 0, 0)
    new, coeff, triangle = call(
        functools.partial(finish_kernel, entries),
        [(STEPS, tiles, 8, span_z), (EARLIER, STEPS), (STEPS, STEPS)],
        1 << 20,
        rows.reshape(devices // 8, 8, span_z),
        basis,
        *columns,
    )
    return new.reshape((STEPS,) + field), coeff, triangle


def solution(mesh):
    in_specs = (
        P(None, None, "gx", "gy", "gz"),
        P(None, "gx", "gy", "gz"),
        P(None, None, "gx", "gy", "gz"),
    )
    out_specs = (P(None, None, "gx", "gy", "gz"), P(), P())
    return jax.shard_map(
        on_device, mesh=mesh, in_specs=in_specs, out_specs=out_specs, check_vma=False
    )
```

time: 281 us -> 80.5 us (0.29)
  blocking collectives: 156 us -> 22.6 us
  other arithmetic: 42.2 us -> 0 us
  waiting for transfers between devices: 31.4 us -> 5.48 us
  starting transfers between devices: 17.9 us -> 42.3 us
  local copies, waits for them, and re-layouts: 23.7 us -> 2.79 us
  matrix products: 8.16 us -> 0 us
  Pallas kernels: 0 us -> 6.37 us
    psum x2 -> x0, blocking collectives: 156 us -> none  [the longest x1 83.7 us: on_device(): lax.psum(jnp.dot(flat_basis, flat_block.T, precision=HIGHEST), ('gx', 'gy...]
    ppermute x6 -> x24, waiting for transfers between devices: 31.4 us -> 5.48 us  [exchange(): halos += [lax.ppermute(high, axis, up), lax.ppermute(low, axis, down)]]
    ppermute x6 -> x24, starting transfers between devices: 17.9 us -> 42.3 us  [exchange(): halos += [lax.ppermute(high, axis, up), lax.ppermute(low, axis, down)]]
    all_to_all x0 -> x1, blocking collectives: none -> 22.6 us  [on_device(): rows = lax.all_to_all(rows.reshape(devices, 1, span_z), AXES, 0, 0)]
    concatenate x4 -> x0, other arithmetic: 21.8 us -> none  [the longest x3 20.6 us: with_halo(): block = jnp.concatenate([low, block, high], axis=dim)]
    mul x10 -> x0, other arithmetic: 16.9 us -> none  [the longest x8 16.7 us: on_device(): (applied - SHIFTS[degree] * center) * DAMPING]
    slice x7 -> x0, local copies, waits for them, and re-layouts: 12.2 us -> none  [the longest x2 7.45 us: with_halo(): lax.slice_in_dim(block, block.shape[dim] - width, None, axis=dim)]
    dot_general x3 -> x0, matrix products: 6.95 us -> none  [the longest x1 2.74 us: on_device(): jnp.dot(flat_basis, flat_block.T, precision=HIGHEST)]
  transfers between devices with their start and end apart: 6 -> 24, of which waited for: 5 -> 7; matrix products, arithmetic and copies ran while one was open for 4% -> 0% of each run, Pallas kernels for 0% -> 3%
where the time goes in v1:
time: 80.5 us; the launch traced here: 80.3 us
  starting transfers between devices  42.3 us (53%)
  blocking collectives  22.6 us (28%)
  Pallas kernels  6.37 us (8%)
  waiting for transfers between devices  5.48 us (7%)
  local copies, waits for them, and re-layouts  2.79 us (3%)
    ppermute x24, starting transfers between devices, exchange(): halos += [lax.ppermute(high, axis, up), lax.ppermute(low, axis, down)]  42.3 us
    all_to_all x1, blocking collectives, on_device(): rows = lax.all_to_all(rows.reshape(devices, 1, span_z), AXES, 0, 0)  22.6 us
    pallas_call x10, Pallas kernels, call(): pl.pallas_call(body, out_shape=[jax.ShapeDtypeStruct(shape, jnp.float32)...  6.37 us
    ppermute x24, waiting for transfers between devices, exchange(): halos += [lax.ppermute(high, axis, up), lax.ppermute(low, axis, down)]  5.48 us
    unnamed x11, local copies, waits for them, and re-layouts  2.79 us
  transfers between devices with their start and end apart: 24, of which 7 were waited for; matrix products, arithmetic and copies ran while one was open for 0% of the time, Pallas kernels for 3%

profile of v1, /device:TPU:1, one launch (start us, length us, event | category | flops | bytes accessed | tf_op | source)
XLA Modules:
  0.0 80.3 jit_solution(12391417592902096346)
XLA Ops:
  0.6 1.2 %copy-done = f32[8,4,4,16,128]{4,3,2,1,0:T(8,128)S(1)} copy-done((f32[8,4,4,16,128]{4,3,2,1,0:T(8,128)S(1)}, f32[8,4,4,16,128]{4,3,2,1,0:T(8,128)}, u32[]{:S(2)}) %copy-start) | copy-done | bytes 1048600
  1.9 0.9 %copy-done.3 = f32[4,4,16,128]{3,2,1,0:T(8,128)S(1)} copy-done((f32[4,4,16,128]{3,2,1,0:T(8,128)S(1)}, f32[4,4,16,128]{3,2,1,0:T(8,128)}, u32[]{:S(2)}) %copy-start.3) | copy-done | bytes 131096
  3.0 2.1 %collective-permute-start = (f32[8,16,128]{2,1,0:T(8,128)S(1)}, f32[8,16,128]{2,1,0:T(8,128)S(1)}, u32[]{:S(2)}, u32[]{:S(2)}) collective-permute-start(f32[8,16,128]{2,1,0:T(8,128)S(1)} %get-tuple-element.35), channel_id=1, source_target_pairs={{0,64},{64,128},{128,192},{192,0},{1,65},{65,129},{129,193},{193,1... | collective-permute-start | bytes 196616 | tf_op jit(solution)/shard_map/ppermute | solution.py:258
  5.1 1.4 %collective-permute-start.1 = (f32[8,16,128]{2,1,0:T(8,128)S(1)}, f32[8,16,128]{2,1,0:T(8,128)S(1)}, u32[]{:S(2)}, u32[]{:S(2)}) collective-permute-start(f32[8,16,128]{2,1,0:T(8,128)S(1)} %get-tuple-element.36), channel_id=1, source_target_pairs={{64,0},{128,64},{192,128},{0,192},{65,1},{129,65},{193,129},{1,193... | collective-permute-start | bytes 196616 | tf_op jit(solution)/shard_map/ppermute | solution.py:258
  6.4 1.7 %collective-permute-start.4 = (f32[16,128]{1,0:T(8,128)S(1)}, f32[16,128]{1,0:T(8,128)S(1)}, u32[]{:S(2)}, u32[]{:S(2)}) collective-permute-start(f32[16,128]{1,0:T(8,128)S(1)} %get-tuple-element.39), channel_id=1, source_target_pairs={{0,1},{1,2},{2,3},{3,4},{4,5},{5,6},{6,7},{7,0},{8,9},{9,10},{10,1... | collective-permute-start | bytes 24584 | tf_op jit(solution)/shard_map/ppermute | solution.py:258
  8.2 2.7 %collective-permute-start.2 = (f32[32,128]{1,0:T(8,128)S(1)}, f32[32,128]{1,0:T(8,128)S(1)}, u32[]{:S(2)}, u32[]{:S(2)}) collective-permute-start(f32[32,128]{1,0:T(8,128)S(1)} %get-tuple-element.37), channel_id=1, source_target_pairs={{0,8},{8,16},{16,24},{24,32},{32,40},{40,48},{48,56},{56,0},{1,9},... | collective-permute-start | bytes 49160 | tf_op jit(solution)/shard_map/ppermute | solution.py:258
  10.9 2.3 %collective-permute-done.4.refs_7_ = f32[16,128]{1,0:T(8,128)S(1)} collective-permute-done((f32[16,128]{1,0:T(8,128)S(1)}, f32[16,128]{1,0:T(8,128)S(1)}, u32[]{:S(2)}, u32[]{:S(2)}) %collective-permute-start.4) | collective-permute-done | bytes 8224 | tf_op jit(solution)/shard_map/ppermute | solution.py:258
  13.2 1.8 %collective-permute-start.5 = (f32[16,128]{1,0:T(8,128)S(1)}, f32[16,128]{1,0:T(8,128)S(1)}, u32[]{:S(2)}, u32[]{:S(2)}) collective-permute-start(f32[16,128]{1,0:T(8,128)S(1)} %get-tuple-element.40), channel_id=1, source_target_pairs={{1,0},{2,1},{3,2},{4,3},{5,4},{6,5},{7,6},{0,7},{9,8},{10,9},{11,1... | collective-permute-start | bytes 24584 | tf_op jit(solution)/shard_map/ppermute | solution.py:258
  14.9 0.8 collective-permute-done.5.refs_8_
  16.3 2.7 %collective-permute-start.7 = (f32[4,16,128]{2,1,0:T(8,128)S(1)}, f32[4,16,128]{2,1,0:T(8,128)S(1)}, u32[]{:S(2)}, u32[]{:S(2)}) collective-permute-start(f32[4,16,128]{2,1,0:T(8,128)S(1)} %get-tuple-element.43), channel_id=1, source_target_pairs={{64,0},{128,64},{192,128},{0,192},{65,1},{129,65},{193,129},{1,193... | collective-permute-start | bytes 98312 | tf_op jit(solution)/shard_map/ppermute | solution.py:258
  18.9 4.9 %collective-permute-start.8 = (f32[16,128]{1,0:T(8,128)S(1)}, f32[16,128]{1,0:T(8,128)S(1)}, u32[]{:S(2)}, u32[]{:S(2)}) collective-permute-start(f32[16,128]{1,0:T(8,128)S(1)} %get-tuple-element.44), channel_id=1, source_target_pairs={{0,8},{8,16},{16,24},{24,32},{32,40},{40,48},{48,56},{56,0},{1,9},... | collective-permute-start | bytes 24584 | tf_op jit(solution)/shard_map/ppermute | solution.py:258
  24.7 3.0 %collective-permute-start.11 = (f32[16,128]{1,0:T(8,128)S(1)}, f32[16,128]{1,0:T(8,128)S(1)}, u32[]{:S(2)}, u32[]{:S(2)}) collective-permute-start(f32[16,128]{1,0:T(8,128)S(1)} %get-tuple-element.47), channel_id=1, source_target_pairs={{1,0},{2,1},{3,2},{4,3},{5,4},{6,5},{7,6},{0,7},{9,8},{10,9},{11,1... | collective-permute-start | bytes 24584 | tf_op jit(solution)/shard_map/ppermute | solution.py:258
  29.0 2.7 %collective-permute-start.13 = (f32[4,16,128]{2,1,0:T(8,128)S(1)}, f32[4,16,128]{2,1,0:T(8,128)S(1)}, u32[]{:S(2)}, u32[]{:S(2)}) collective-permute-start(f32[4,16,128]{2,1,0:T(8,128)S(1)} %get-tuple-element.50), channel_id=1, source_target_pairs={{64,0},{128,64},{192,128},{0,192},{65,1},{129,65},{193,129},{1,193... | collective-permute-start | bytes 98312 | tf_op jit(solution)/shard_map/ppermute | solution.py:258
  31.7 3.7 %collective-permute-start.14 = (f32[16,128]{1,0:T(8,128)S(1)}, f32[16,128]{1,0:T(8,128)S(1)}, u32[]{:S(2)}, u32[]{:S(2)}) collective-permute-start(f32[16,128]{1,0:T(8,128)S(1)} %get-tuple-element.51), channel_id=1, source_target_pairs={{0,8},{8,16},{16,24},{24,32},{32,40},{40,48},{48,56},{56,0},{1,9},... | collective-permute-start | bytes 24584 | tf_op jit(solution)/shard_map/ppermute | solution.py:258
  35.4 1.0 %collective-permute-start.16 = (f32[16,128]{1,0:T(8,128)S(1)}, f32[16,128]{1,0:T(8,128)S(1)}, u32[]{:S(2)}, u32[]{:S(2)}) collective-permute-start(f32[16,128]{1,0:T(8,128)S(1)} %get-tuple-element.53), channel_id=1, source_target_pairs={{0,1},{1,2},{2,3},{3,4},{4,5},{5,6},{6,7},{7,0},{8,9},{9,10},{10,1... | collective-permute-start | bytes 24584 | tf_op jit(solution)/shard_map/ppermute | solution.py:258
  36.4 3.0 %collective-permute-start.17 = (f32[16,128]{1,0:T(8,128)S(1)}, f32[16,128]{1,0:T(8,128)S(1)}, u32[]{:S(2)}, u32[]{:S(2)}) collective-permute-start(f32[16,128]{1,0:T(8,128)S(1)} %get-tuple-element.54), channel_id=1, source_target_pairs={{1,0},{2,1},{3,2},{4,3},{5,4},{6,5},{7,6},{0,7},{9,8},{10,9},{11,1... | collective-permute-start | bytes 24584 | tf_op jit(solution)/shard_map/ppermute | solution.py:258
  40.7 2.7 %collective-permute-start.19 = (f32[4,16,128]{2,1,0:T(8,128)S(1)}, f32[4,16,128]{2,1,0:T(8,128)S(1)}, u32[]{:S(2)}, u32[]{:S(2)}) collective-permute-start(f32[4,16,128]{2,1,0:T(8,128)S(1)} %get-tuple-element.57), channel_id=1, source_target_pairs={{64,0},{128,64},{192,128},{0,192},{65,1},{129,65},{193,129},{1,193... | collective-permute-start | bytes 98312 | tf_op jit(solution)/shard_map/ppermute | solution.py:258
  43.4 3.7 %collective-permute-start.20 = (f32[16,128]{1,0:T(8,128)S(1)}, f32[16,128]{1,0:T(8,128)S(1)}, u32[]{:S(2)}, u32[]{:S(2)}) collective-permute-start(f32[16,128]{1,0:T(8,128)S(1)} %get-tuple-element.58), channel_id=1, source_target_pairs={{0,8},{8,16},{16,24},{24,32},{32,40},{40,48},{48,56},{56,0},{1,9},... | collective-permute-start | bytes 24584 | tf_op jit(solution)/shard_map/ppermute | solution.py:258
  47.1 1.2 %collective-permute-start.21 = (f32[16,128]{1,0:T(8,128)S(1)}, f32[16,128]{1,0:T(8,128)S(1)}, u32[]{:S(2)}, u32[]{:S(2)}) collective-permute-start(f32[16,128]{1,0:T(8,128)S(1)} %get-tuple-element.59), channel_id=1, source_target_pairs={{8,0},{16,8},{24,16},{32,24},{40,32},{48,40},{56,48},{0,56},{9,1},... | collective-permute-start | bytes 24584 | tf_op jit(solution)/shard_map/ppermute | solution.py:258
  48.3 1.0 %collective-permute-start.22 = (f32[16,128]{1,0:T(8,128)S(1)}, f32[16,128]{1,0:T(8,128)S(1)}, u32[]{:S(2)}, u32[]{:S(2)}) collective-permute-start(f32[16,128]{1,0:T(8,128)S(1)} %get-tuple-element.60), channel_id=1, source_target_pairs={{0,1},{1,2},{2,3},{3,4},{4,5},{5,6},{6,7},{7,0},{8,9},{9,10},{10,1... | collective-permute-start | bytes 24584 | tf_op jit(solution)/shard_map/ppermute | solution.py:258
  49.3 2.9 %collective-permute-start.23 = (f32[16,128]{1,0:T(8,128)S(1)}, f32[16,128]{1,0:T(8,128)S(1)}, u32[]{:S(2)}, u32[]{:S(2)}) collective-permute-start(f32[16,128]{1,0:T(8,128)S(1)} %get-tuple-element.61), channel_id=1, source_target_pairs={{1,0},{2,1},{3,2},{4,3},{5,4},{6,5},{7,6},{0,7},{9,8},{10,9},{11,1... | collective-permute-start | bytes 24584 | tf_op jit(solution)/shard_map/ppermute | solution.py:258
  54.3 0.9 %shard_map.66 = (f32[32,8,128]{2,1,0:T(8,128)S(1)}, f32[256,128]{1,0:T(8,128)S(1)}) custom-call(f32[4,4,16,128]{3,2,1,0:T(8,128)S(1)} %get-tuple-element.55.refs_0_, f32[4,4,16,128]{3,2,1,0:T(8,128)S(1)} %copy-done.4, f32[4,4,4,16,128]{4,3,2,1,0:T(8,128)S(1)} %copy-done.2, f32[8,16,128]{2,1,0:T(8,128)S(1)} %collective-permute-done.refs_3_, ...), custom_call_target="tpu_custom_call" | custom-call | flops 1048576 | bytes 1048576 | tf_op jit(solution)/shard_map/pallas_call | solution.py:242
  55.1 22.6 %all_to_all.5 = f32[256,1,128]{2,1,0:T(1,128)S(1)} all-to-all(f32[256,1,128]{2,1,0:T(1,128)S(1)} %bitcast.27), channel_id=1, replica_groups=mesh['gx'=4,'gy'=8,'gz'=8] {'gx','gy','gz'}, dimensions={0} | all-to-all | bytes 262144 | tf_op jit(solution)/shard_map/all_to_all | solution.py:346
  77.8 1.9 %shard_map.67 = (f32[4,32,8,128]{3,2,1,0:T(8,128)}, f32[8,4]{1,0:T(8,128)S(1)}, f32[4,4]{1,0:T(4,128)}) custom-call(f32[32,8,128]{2,1,0:T(8,128)S(1)} %bitcast.26, f32[8,32,8,128]{3,2,1,0:T(8,128)S(1)} %bitcast.14, f32[32,8,128]{2,1,0:T(8,128)S(1)} %bitcast.19, f32[32,8,128]{2,1,0:T(8,128)S(1)} %bitcast.23, f32[32,8,128]{2,1,0:T(8,128)S(1)} %bitcast.25, ...), custom_call_target="tpu_custom_call" | custom-call | flops 1048576 | bytes 1048576 | tf_op jit(solution)/shard_map/pallas_call | solution.py:242
  (46 shorter events, 6.9 us)
Async XLA Ops:
  3.0 12.8 %collective-permute-start = (f32[8,16,128]{2,1,0:T(8,128)S(1)}, f32[8,16,128]{2,1,0:T(8,128)S(1)}, u32[]{:S(2)}, u32[]{:S(2)}) collective-permute-start(f32[8,16,128]{2,1,0:T(8,128)S(1)} %get-tuple-element.35), channel_id=1, source_target_pairs={{0,64},{64,128},{128,192},{192,0},{1,65},{65,129},{129,193},{193,1... | collective-permute-start | bytes 196616 | tf_op jit(solution)/shard_map/ppermute | solution.py:258
  5.1 10.6 %collective-permute-start.1 = (f32[8,16,128]{2,1,0:T(8,128)S(1)}, f32[8,16,128]{2,1,0:T(8,128)S(1)}, u32[]{:S(2)}, u32[]{:S(2)}) collective-permute-start(f32[8,16,128]{2,1,0:T(8,128)S(1)} %get-tuple-element.36), channel_id=1, source_target_pairs={{64,0},{128,64},{192,128},{0,192},{65,1},{129,65},{193,129},{1,193... | collective-permute-start | bytes 196616 | tf_op jit(solution)/shard_map/ppermute | solution.py:258
  6.4 6.7 %collective-permute-start.4 = (f32[16,128]{1,0:T(8,128)S(1)}, f32[16,128]{1,0:T(8,128)S(1)}, u32[]{:S(2)}, u32[]{:S(2)}) collective-permute-start(f32[16,128]{1,0:T(8,128)S(1)} %get-tuple-element.39), channel_id=1, source_target_pairs={{0,1},{1,2},{2,3},{3,4},{4,5},{5,6},{6,7},{7,0},{8,9},{9,10},{10,1... | collective-permute-start | bytes 24584 | tf_op jit(solution)/shard_map/ppermute | solution.py:258
  8.2 7.5 %collective-permute-start.2 = (f32[32,128]{1,0:T(8,128)S(1)}, f32[32,128]{1,0:T(8,128)S(1)}, u32[]{:S(2)}, u32[]{:S(2)}) collective-permute-start(f32[32,128]{1,0:T(8,128)S(1)} %get-tuple-element.37), channel_id=1, source_target_pairs={{0,8},{8,16},{16,24},{24,32},{32,40},{40,48},{48,56},{56,0},{1,9},... | collective-permute-start | bytes 49160 | tf_op jit(solution)/shard_map/ppermute | solution.py:258
  10.9 4.8 %collective-permute-start.3 = (f32[32,128]{1,0:T(8,128)S(1)}, f32[32,128]{1,0:T(8,128)S(1)}, u32[]{:S(2)}, u32[]{:S(2)}) collective-permute-start(f32[32,128]{1,0:T(8,128)S(1)} %get-tuple-element.38), channel_id=1, source_target_pairs={{8,0},{16,8},{24,16},{32,24},{40,32},{48,40},{56,48},{0,56},{9,1},... | collective-permute-start | bytes 49160 | tf_op jit(solution)/shard_map/ppermute | solution.py:258
  13.2 2.6 %collective-permute-start.5 = (f32[16,128]{1,0:T(8,128)S(1)}, f32[16,128]{1,0:T(8,128)S(1)}, u32[]{:S(2)}, u32[]{:S(2)}) collective-permute-start(f32[16,128]{1,0:T(8,128)S(1)} %get-tuple-element.40), channel_id=1, source_target_pairs={{1,0},{2,1},{3,2},{4,3},{5,4},{6,5},{7,6},{0,7},{9,8},{10,9},{11,1... | collective-permute-start | bytes 24584 | tf_op jit(solution)/shard_map/ppermute | solution.py:258
  16.2 12.2 %collective-permute-start.6 = (f32[4,16,128]{2,1,0:T(8,128)S(1)}, f32[4,16,128]{2,1,0:T(8,128)S(1)}, u32[]{:S(2)}, u32[]{:S(2)}) collective-permute-start(f32[4,16,128]{2,1,0:T(8,128)S(1)} %get-tuple-element.42), channel_id=1, source_target_pairs={{0,64},{64,128},{128,192},{192,0},{1,65},{65,129},{129,193},{193,1... | collective-permute-start | bytes 98312 | tf_op jit(solution)/shard_map/ppermute | solution.py:258
  16.3 12.2 %collective-permute-start.7 = (f32[4,16,128]{2,1,0:T(8,128)S(1)}, f32[4,16,128]{2,1,0:T(8,128)S(1)}, u32[]{:S(2)}, u32[]{:S(2)}) collective-permute-start(f32[4,16,128]{2,1,0:T(8,128)S(1)} %get-tuple-element.43), channel_id=1, source_target_pairs={{64,0},{128,64},{192,128},{0,192},{65,1},{129,65},{193,129},{1,193... | collective-permute-start | bytes 98312 | tf_op jit(solution)/shard_map/ppermute | solution.py:258
  18.9 5.7 %collective-permute-start.8 = (f32[16,128]{1,0:T(8,128)S(1)}, f32[16,128]{1,0:T(8,128)S(1)}, u32[]{:S(2)}, u32[]{:S(2)}) collective-permute-start(f32[16,128]{1,0:T(8,128)S(1)} %get-tuple-element.44), channel_id=1, source_target_pairs={{0,8},{8,16},{16,24},{24,32},{32,40},{40,48},{48,56},{56,0},{1,9},... | collective-permute-start | bytes 24584 | tf_op jit(solution)/shard_map/ppermute | solution.py:258
  23.9 3.7 %collective-permute-start.9 = (f32[16,128]{1,0:T(8,128)S(1)}, f32[16,128]{1,0:T(8,128)S(1)}, u32[]{:S(2)}, u32[]{:S(2)}) collective-permute-start(f32[16,128]{1,0:T(8,128)S(1)} %get-tuple-element.45), channel_id=1, source_target_pairs={{8,0},{16,8},{24,16},{32,24},{40,32},{48,40},{56,48},{0,56},{9,1},... | collective-permute-start | bytes 24584 | tf_op jit(solution)/shard_map/ppermute | solution.py:258
  23.9 4.0 %collective-permute-start.10 = (f32[16,128]{1,0:T(8,128)S(1)}, f32[16,128]{1,0:T(8,128)S(1)}, u32[]{:S(2)}, u32[]{:S(2)}) collective-permute-start(f32[16,128]{1,0:T(8,128)S(1)} %get-tuple-element.46), channel_id=1, source_target_pairs={{0,1},{1,2},{2,3},{3,4},{4,5},{5,6},{6,7},{7,0},{8,9},{9,10},{10,1... | collective-permute-start | bytes 24584 | tf_op jit(solution)/shard_map/ppermute | solution.py:258
  24.7 3.7 %collective-permute-start.11 = (f32[16,128]{1,0:T(8,128)S(1)}, f32[16,128]{1,0:T(8,128)S(1)}, u32[]{:S(2)}, u32[]{:S(2)}) collective-permute-start(f32[16,128]{1,0:T(8,128)S(1)} %get-tuple-element.47), channel_id=1, source_target_pairs={{1,0},{2,1},{3,2},{4,3},{5,4},{6,5},{7,6},{0,7},{9,8},{10,9},{11,1... | collective-permute-start | bytes 24584 | tf_op jit(solution)/shard_map/ppermute | solution.py:258
  28.9 11.2 %collective-permute-start.12 = (f32[4,16,128]{2,1,0:T(8,128)S(1)}, f32[4,16,128]{2,1,0:T(8,128)S(1)}, u32[]{:S(2)}, u32[]{:S(2)}) collective-permute-start(f32[4,16,128]{2,1,0:T(8,128)S(1)} %get-tuple-element.49), channel_id=1, source_target_pairs={{0,64},{64,128},{128,192},{192,0},{1,65},{65,129},{129,193},{193,1... | collective-permute-start | bytes 98312 | tf_op jit(solution)/shard_map/ppermute | solution.py:258
  29.0 11.2 %collective-permute-start.13 = (f32[4,16,128]{2,1,0:T(8,128)S(1)}, f32[4,16,128]{2,1,0:T(8,128)S(1)}, u32[]{:S(2)}, u32[]{:S(2)}) collective-permute-start(f32[4,16,128]{2,1,0:T(8,128)S(1)} %get-tuple-element.50), channel_id=1, source_target_pairs={{64,0},{128,64},{192,128},{0,192},{65,1},{129,65},{193,129},{1,193... | collective-permute-start | bytes 98312 | tf_op jit(solution)/shard_map/ppermute | solution.py:258
  31.7 4.7 %collective-permute-start.14 = (f32[16,128]{1,0:T(8,128)S(1)}, f32[16,128]{1,0:T(8,128)S(1)}, u32[]{:S(2)}, u32[]{:S(2)}) collective-permute-start(f32[16,128]{1,0:T(8,128)S(1)} %get-tuple-element.51), channel_id=1, source_target_pairs={{0,8},{8,16},{16,24},{24,32},{32,40},{40,48},{48,56},{56,0},{1,9},... | collective-permute-start | bytes 24584 | tf_op jit(solution)/shard_map/ppermute | solution.py:258
  35.4 4.0 %collective-permute-start.15 = (f32[16,128]{1,0:T(8,128)S(1)}, f32[16,128]{1,0:T(8,128)S(1)}, u32[]{:S(2)}, u32[]{:S(2)}) collective-permute-start(f32[16,128]{1,0:T(8,128)S(1)} %get-tuple-element.52), channel_id=1, source_target_pairs={{8,0},{16,8},{24,16},{32,24},{40,32},{48,40},{56,48},{0,56},{9,1},... | collective-permute-start | bytes 24584 | tf_op jit(solution)/shard_map/ppermute | solution.py:258
  35.4 4.3 %collective-permute-start.16 = (f32[16,128]{1,0:T(8,128)S(1)}, f32[16,128]{1,0:T(8,128)S(1)}, u32[]{:S(2)}, u32[]{:S(2)}) collective-permute-start(f32[16,128]{1,0:T(8,128)S(1)} %get-tuple-element.53), channel_id=1, source_target_pairs={{0,1},{1,2},{2,3},{3,4},{4,5},{5,6},{6,7},{7,0},{8,9},{9,10},{10,1... | collective-permute-start | bytes 24584 | tf_op jit(solution)/shard_map/ppermute | solution.py:258
  36.4 3.8 %collective-permute-start.17 = (f32[16,128]{1,0:T(8,128)S(1)}, f32[16,128]{1,0:T(8,128)S(1)}, u32[]{:S(2)}, u32[]{:S(2)}) collective-permute-start(f32[16,128]{1,0:T(8,128)S(1)} %get-tuple-element.54), channel_id=1, source_target_pairs={{1,0},{2,1},{3,2},{4,3},{5,4},{6,5},{7,6},{0,7},{9,8},{10,9},{11,1... | collective-permute-start | bytes 24584 | tf_op jit(solution)/shard_map/ppermute | solution.py:258
  40.6 13.6 %collective-permute-start.18 = (f32[4,16,128]{2,1,0:T(8,128)S(1)}, f32[4,16,128]{2,1,0:T(8,128)S(1)}, u32[]{:S(2)}, u32[]{:S(2)}) collective-permute-start(f32[4,16,128]{2,1,0:T(8,128)S(1)} %get-tuple-element.56), channel_id=1, source_target_pairs={{0,64},{64,128},{128,192},{192,0},{1,65},{65,129},{129,193},{193,1... | collective-permute-start | bytes 98312 | tf_op jit(solution)/shard_map/ppermute | solution.py:258
  40.7 13.6 %collective-permute-start.19 = (f32[4,16,128]{2,1,0:T(8,128)S(1)}, f32[4,16,128]{2,1,0:T(8,128)S(1)}, u32[]{:S(2)}, u32[]{:S(2)}) collective-permute-start(f32[4,16,128]{2,1,0:T(8,128)S(1)} %get-tuple-element.57), channel_id=1, source_target_pairs={{64,0},{128,64},{192,128},{0,192},{65,1},{129,65},{193,129},{1,193... | collective-permute-start | bytes 98312 | tf_op jit(solution)/shard_map/ppermute | solution.py:258
  43.4 5.9 %collective-permute-start.20 = (f32[16,128]{1,0:T(8,128)S(1)}, f32[16,128]{1,0:T(8,128)S(1)}, u32[]{:S(2)}, u32[]{:S(2)}) collective-permute-start(f32[16,128]{1,0:T(8,128)S(1)} %get-tuple-element.58), channel_id=1, source_target_pairs={{0,8},{8,16},{16,24},{24,32},{32,40},{40,48},{48,56},{56,0},{1,9},... | collective-permute-start | bytes 24584 | tf_op jit(solution)/shard_map/ppermute | solution.py:258
  47.1 7.1 %collective-permute-start.21 = (f32[16,128]{1,0:T(8,128)S(1)}, f32[16,128]{1,0:T(8,128)S(1)}, u32[]{:S(2)}, u32[]{:S(2)}) collective-permute-start(f32[16,128]{1,0:T(8,128)S(1)} %get-tuple-element.59), channel_id=1, source_target_pairs={{8,0},{16,8},{24,16},{32,24},{40,32},{48,40},{56,48},{0,56},{9,1},... | collective-permute-start | bytes 24584 | tf_op jit(solution)/shard_map/ppermute | solution.py:258
  48.3 5.9 %collective-permute-start.22 = (f32[16,128]{1,0:T(8,128)S(1)}, f32[16,128]{1,0:T(8,128)S(1)}, u32[]{:S(2)}, u32[]{:S(2)}) collective-permute-start(f32[16,128]{1,0:T(8,128)S(1)} %get-tuple-element.60), channel_id=1, source_target_pairs={{0,1},{1,2},{2,3},{3,4},{4,5},{5,6},{6,7},{7,0},{8,9},{9,10},{10,1... | collective-permute-start | bytes 24584 | tf_op jit(solution)/shard_map/ppermute | solution.py:258
  49.3 4.9 %collective-permute-start.23 = (f32[16,128]{1,0:T(8,128)S(1)}, f32[16,128]{1,0:T(8,128)S(1)}, u32[]{:S(2)}, u32[]{:S(2)}) collective-permute-start(f32[16,128]{1,0:T(8,128)S(1)} %get-tuple-element.61), channel_id=1, source_target_pairs={{1,0},{2,1},{3,2},{4,3},{5,4},{6,5},{7,6},{0,7},{9,8},{10,9},{11,1... | collective-permute-start | bytes 24584 | tf_op jit(solution)/shard_map/ppermute | solution.py:258
  (5 other events, 54.1 us)
